TPU v7x, 256 devices: a whole 4x4x8 slice. The times are simulated.
256 devices in a mesh: seq: 16 (over z, core), head: 16 (over y, x).
Axes of the slice: x: 4, y: 4, z: 8, core: 2. Of those that a mesh axis runs over, the one named last changes fastest.
Arguments:
- projections: bfloat16 [49152, 8, 384], P(('seq', 'head')), may hold values from -8 to 8
- routed_heads: int32 [49152, 8], P(('seq', 'head')), may hold values from 0 to 63, as said below
- slot_index: int32 [49152, 8], P(('seq', 'head')), may hold values from 0 to 47, as said below
- gate_logits: float32 [49152, 8], P(('seq', 'head')), may hold values from -8 to 8
- doc_lengths: int32 [32], replicated, may hold values from 1 to 3072, 49152 in all
- cotangent: bfloat16 [49152, 8, 128], P(('seq', 'head')), may hold values from -6 to 6
Outputs:
- head_outputs: bfloat16 [49152, 8, 128], P(('seq', 'head'))
- projection_grads: bfloat16 [49152, 8, 384], P(('seq', 'head'))
- gate_grads: float32 [49152, 8], P(('seq', 'head'))
Inputs may be any that keep to these rules, and one draw needn't show every extreme that they name: `routed_heads`: each token names 8 different heads. Among the 192 tokens of one aligned block at most 48 name the same head, and in every aligned run of 3072 tokens one head is named by exactly 48 tokens of each of its aligned blocks of 192. slot_index[t, k] is the number of tokens before t in t's aligned block of 192 tokens that name head routed_heads[t, k]. `doc_lengths`: the documents lie in order and together fill the 49152 positions.
All inputs are finite; a program needn't handle non-finite values.
Results may differ from a plain program's by a relative error of at most 0.011.
Values may be sent and summed in bfloat16 or wider, within the bound.
A program may use at most 64 MiB of HBM per device.

v0:
```python
import math

import jax
import jax.numpy as jnp
from jax import lax
from jax.experimental import pallas as pl
from jax.experimental.pallas import tpu as pltpu
from jax.sharding import PartitionSpec as P

H = 64
CAP = 48
OWN = 4
PEERS = 16
SPAN = PEERS * CAP
HS = 128
WIDE = 4 * HS
QT = 256
WIN = 1152
KC = 384
MASKED = -1e30
F32 = jnp.float32
BF16 = jnp.bfloat16
MESH = pl.DeviceIdType.MESH


def dot_nt(a, b):
    return lax.dot_general(a, b, (((1,), (1,)), ((), ())), preferred_element_type=F32)


def dot(a, b):
    return jnp.dot(a, b, preferred_element_type=F32)


def one_hot(mask):
    return jnp.where(mask, 1.0, 0.0).astype(BF16)


def thirds(v):
    high = v.astype(BF16).astype(F32)
    middle = (v - high).astype(BF16).astype(F32)
    return [high, middle, v - high - middle]


def dest_weight(f):
    return jnp.where(f < 8, float(CAP), jnp.where(f < 16, 1.0, 0.0)).astype(BF16)


def div48(v):
    return (v * 1366) >> 16


def token_rows(c, tokens):
    r = lax.broadcasted_iota(jnp.int32, (256, tokens), 0)
    t = lax.broadcasted_iota(jnp.int32, (256, tokens), 1)
    return one_hot((r >> 3) + c * 32 == t)


def slot_rows(dest, a):
    lane = lax.broadcasted_iota(jnp.int32, (8, SPAN), 1)
    source = div48(lane)
    ids = (source * (OWN * CAP) + (lane - source * CAP) + a * CAP).astype(F32)
    return one_hot(jnp.concatenate([dest] * (SPAN // 128), axis=1) == ids[0:1, :])


def kernel(
    proj_hbm,
    cot_hbm,
    heads_ref,
    slots_ref,
    logits_ref,
    lengths_hbm,
    routes_out,
    last_out,
    dest_out,
    gate_out,
    lengths_ref,
    x_proj,
    x_cot,
    x_grad,
    dest_ref,
    gate_ref,
    rows_ref,
    out_acc,
    fsend,
    frecv,
    doc_send,
    doc_recv,
    doc_prev,
    kv_prev,
    dsend,
    drecv,
    rsend,
    rrecv,
    k_all,
    v_all,
    k_t,
    v_t,
    key_docs,
    query_docs,
    s_buf,
    p_buf,
    ds_buf,
    dk_acc,
    dv_acc,
    f_ssem,
    f_rsem,
    doc_ssem,
    doc_rsem,
    dp_sem,
    kv_ssem,
    kv_rsem,
    d_ssem,
    d_rsem,
    r_ssem,
    r_rsem,
    in_sem,
    out_sem,
):
    me = lax.axis_index("head")
    here = lax.axis_index("seq")
    after = lax.rem(here + 1, PEERS)
    before = lax.rem(here + PEERS - 1, PEERS)
    routes = proj_hbm.shape[0]
    tokens = heads_ref.shape[1]
    tiles = routes // 128
    scaling = HS ** (-0.5)
    proj_in = pltpu.make_async_copy(proj_hbm, x_proj, in_sem.at[0])
    cot_in = pltpu.make_async_copy(cot_hbm, x_cot, in_sem.at[1])
    lengths_in = pltpu.make_async_copy(lengths_hbm, lengths_ref, in_sem.at[2])
    cot_in.start()
    proj_in.start()
    lengths_in.start()

    barrier = pltpu.get_barrier_semaphore()

    def peer_of(d):
        px = lax.rem(lax.rem(me, 4) + lax.rem(d, 4), 4)
        py = lax.rem(me // 4 + d // 4, 4)
        return py * 4 + px

    @pl.loop(1, PEERS)
    def _(d):
        pl.semaphore_signal(barrier, inc=1, device_id={"head": peer_of(d)}, device_id_type=MESH)

    pl.semaphore_signal(barrier, inc=1, device_id={"seq": after}, device_id_type=MESH)
    pl.semaphore_signal(barrier, inc=1, device_id={"seq": before}, device_id_type=MESH)

    def block(i):
        return pl.ds(pl.multiple_of(i * CAP, CAP), CAP)

    def fwd_copy(a, d):
        peer = peer_of(d)
        return pltpu.make_async_remote_copy(
            src_ref=fsend.at[a, block(peer)],
            dst_ref=frecv.at[a, block(me)],
            send_sem=f_ssem.at[a, d],
            recv_sem=f_rsem.at[a, d],
            device_id={"head": peer},
            device_id_type=MESH,
        )

    def ret_copy(a, d):
        peer = peer_of(d)
        return pltpu.make_async_remote_copy(
            src_ref=rsend.at[a, block(peer)],
            dst_ref=rrecv.at[a, block(me)],
            send_sem=r_ssem.at[a, d],
            recv_sem=r_rsem.at[a, d],
            device_id={"head": peer},
            device_id_type=MESH,
        )

    def last_copy(d):
        peer = peer_of(d)
        return pltpu.make_async_remote_copy(
            src_ref=rsend.at[OWN - 1, block(peer)],
            dst_ref=last_out.at[block(me)],
            send_sem=r_ssem.at[OWN - 1, d],
            recv_sem=r_rsem.at[OWN - 1, d],
            device_id={"head": peer},
            device_id_type=MESH,
        )

    def doc_rows(i):
        return pl.ds(pl.multiple_of(i * 16, 16), 16)

    def doc_copy(d):
        peer = peer_of(d)
        return pltpu.make_async_remote_copy(
            src_ref=doc_send.at[doc_rows(peer)],
            dst_ref=doc_recv.at[doc_rows(me)],
            send_sem=doc_ssem.at[d],
            recv_sem=doc_rsem.at[d],
            device_id={"head": peer},
            device_id_type=MESH,
        )

    doc_shift = pltpu.make_async_remote_copy(
        src_ref=doc_recv,
        dst_ref=doc_prev,
        send_sem=dp_sem.at[0],
        recv_sem=dp_sem.at[1],
        device_id={"seq": after},
        device_id_type=MESH,
    )

    def kv_copy(a):
        return pltpu.make_async_remote_copy(
            src_ref=frecv.at[a, :, pl.ds(HS, 2 * HS)],
            dst_ref=kv_prev.at[a],
            send_sem=kv_ssem.at[a],
            recv_sem=kv_rsem.at[a],
            device_id={"seq": after},
            device_id_type=MESH,
        )

    def d_copy(a):
        return pltpu.make_async_remote_copy(
            src_ref=dsend.at[a],
            dst_ref=drecv.at[a],
            send_sem=d_ssem.at[a],
            recv_sem=d_rsem.at[a],
            device_id={"seq": before},
            device_id_type=MESH,
        )

    gate = 1.0 / (1.0 + jnp.exp(-logits_ref[...]))
    pieces = thirds(gate)
    fields = jnp.concatenate(
        [heads_ref[...].astype(F32), slots_ref[...].astype(F32)] + pieces, axis=0
    ).astype(BF16)
    count = fields.shape[0]

    for c in range(routes // 256):
        rows = pl.ds(c * 256, 256)
        mixed = dot_nt(token_rows(c, tokens), fields)
        r = lax.broadcasted_iota(jnp.int32, (256, count), 0)
        f = lax.broadcasted_iota(jnp.int32, (256, count), 1)
        mixed = jnp.where((r & 7) == (f & 7), mixed, 0.0).astype(BF16)
        f = lax.broadcasted_iota(jnp.int32, (count, 128), 0)
        dest_ref[rows, :] = dot(mixed, dest_weight(f))
        gate_ref[rows, :] = dot(mixed, one_hot(f >= 16))
        f = lax.broadcasted_iota(jnp.int32, (8, count), 1)
        want = lax.broadcasted_iota(jnp.int32, (8, count), 0)
        as_head = (want == 1) & (f < 8)
        as_slot = (want == 2) & (f >= 8) & (f < 16)
        weight = jnp.where(want == 0, dest_weight(f).astype(F32), jnp.where(as_head | as_slot, 1.0, 0.0))
        rows_ref[:, rows] = dot_nt(weight.astype(BF16), mixed)

    cot_in.wait()
    for c in range(routes // 256):
        rows = pl.ds(c * 256, 256)
        x_grad[rows, :] = (x_cot[rows, :].astype(F32) * gate_ref[rows, :]).astype(BF16)

    proj_in.wait()
    dest_copy = pltpu.make_async_copy(dest_ref, dest_out, out_sem.at[0])
    gate_copy = pltpu.make_async_copy(gate_ref, gate_out, out_sem.at[1])
    dest_copy.start()
    gate_copy.start()

    def dispatch(a, c):
        first = pl.multiple_of(lax.rem(me // 4 + c, 4) * (4 * CAP), 4 * CAP)
        rows = pl.ds(first, 4 * CAP)
        r = lax.broadcasted_iota(jnp.int32, (4 * CAP, 128), 0) + first
        source = div48(r)
        ids = (source * (OWN * CAP) + (r - source * CAP) + a * CAP).astype(F32)
        hot = one_hot(jnp.concatenate([ids] * tiles, axis=1) == rows_ref[0:1, :])
        fsend[a, rows, : 3 * HS] = dot(hot, x_proj[...]).astype(BF16)
        fsend[a, rows, 3 * HS :] = dot(hot, x_grad[...]).astype(BF16)

    def ship(a, c):
        @pl.loop(0, 4)
        def _(x):
            @pl.when(c * 4 + x > 0)
            def _():
                fwd_copy(a, c * 4 + x).start()

    dispatch(0, 0)
    pl.semaphore_wait(barrier, PEERS + 1)
    ship(0, 0)

    @pl.loop(1, 4)
    def _(n):
        dispatch(0, n)
        ship(0, n)

    lane_route = lax.broadcasted_iota(jnp.int32, (8, routes), 1)
    position = (lane_route >> 3) + (here * PEERS + me) * tokens
    docs = jnp.ones((8, routes), F32)
    lengths_in.wait()
    end = lengths_ref[0]
    for n in range(lengths_ref.shape[0]):
        docs = docs + jnp.where(position >= end, 1.0, 0.0)
        if n + 1 < lengths_ref.shape[0]:
            end = end + lengths_ref[n + 1]
    row = lax.broadcasted_iota(jnp.int32, (256, 128), 0)
    row_head = (4 * (row >> 4) + (row & 3)).astype(F32)
    at_head = jnp.concatenate([row_head] * tiles, axis=1) == rows_ref[1:2, :]
    docs_wide = jnp.where(at_head, docs[0:1, :], 0.0).astype(BF16)
    lane_slot = lax.broadcasted_iota(jnp.int32, (128, 128), 0).astype(F32)
    at_slot = one_hot(jnp.concatenate([lane_slot] * tiles, axis=1) == rows_ref[2:3, :])
    doc_send[...] = dot_nt(docs_wide, at_slot).astype(BF16)
    doc_recv[doc_rows(me), :] = doc_send[doc_rows(me), :]

    @pl.loop(1, PEERS)
    def _(d):
        doc_copy(d).start()

    @pl.loop(4, 4 * OWN)
    def _(n):
        dispatch(n >> 2, n & 3)
        ship(n >> 2, n & 3)

    @pl.loop(0, OWN)
    def _(a):
        frecv[a, block(me), :] = fsend[a, block(me), :]

    @pl.loop(1, PEERS)
    def _(d):
        doc_copy(d).wait_recv()

    doc_shift.start()

    def take_head(a):
        @pl.loop(1, PEERS)
        def _(d):
            fwd_copy(a, d).wait_recv()

        kv_copy(a).start()

    def head_docs(a, docs_ref):
        r = lax.broadcasted_iota(jnp.int32, (SPAN, 128), 0)
        lane = lax.broadcasted_iota(jnp.int32, (SPAN, 128), 1)
        source = div48(r)
        wanted = source * 16 + a
        pick = one_hot(jnp.concatenate([lane, lane + 128], axis=1) == jnp.concatenate([wanted] * 2, axis=1))
        spread = dot(pick, docs_ref[...])
        return jnp.where(lane == r - source * CAP, spread, 0.0).astype(BF16)

    def attention(a):
        k_all[:SPAN, :] = kv_prev[a, :, :HS]
        v_all[:SPAN, :] = kv_prev[a, :, HS:]
        k_all[SPAN:, :] = frecv[a, :, HS : 2 * HS]
        v_all[SPAN:, :] = frecv[a, :, 2 * HS : 3 * HS]
        k_t[...] = k_all[...].T
        v_t[...] = v_all[...].T
        ones = jnp.ones((HS, HS), BF16)
        mine = head_docs(a, doc_recv)
        key_docs[:SPAN, :] = dot(head_docs(a, doc_prev), ones)
        key_docs[SPAN:, :] = dot(mine, ones)
        query_docs[...] = dot_nt(ones[:8], mine)
        dk_acc[a] = jnp.zeros((2 * SPAN, HS), F32)
        dv_acc[a] = jnp.zeros((2 * SPAN, HS), F32)

        @pl.loop(0, SPAN // QT)
        def _(i):
            first = pl.multiple_of(i * QT, QT)
            start = pl.multiple_of(((i * (i + 1)) >> 1) * 128, 128)
            q = frecv[a, pl.ds(first, QT), :HS]
            out_grad = frecv[a, pl.ds(first, QT), 3 * HS :]
            q_docs = query_docs[0:1, pl.ds(first, QT)]
            top = jnp.full((1, QT), MASKED, F32)
            for c in range(WIN // KC):
                keys = pl.ds(pl.multiple_of(start + c * KC, 128), KC)
                s = dot_nt(k_all[keys, :], q) * (scaling * math.log2(math.e))
                docs = key_docs[keys, :]
                seen = jnp.concatenate([docs, docs], axis=1) == q_docs
                if (c + 1) * KC > SPAN:
                    k_at = lax.broadcasted_iota(jnp.int32, (KC, QT), 0) + (start + c * KC - SPAN)
                    q_at = lax.broadcasted_iota(jnp.int32, (KC, QT), 1) + first
                    seen = seen & (k_at <= q_at)
                s = jnp.where(seen, s, MASKED)
                s_buf[c * KC : (c + 1) * KC, :] = s
                top = jnp.maximum(top, jnp.max(s, axis=0, keepdims=True))
            total = jnp.zeros((1, QT), F32)
            for c in range(WIN // KC):
                part = slice(c * KC, (c + 1) * KC)
                p = jnp.exp2(s_buf[part, :] - top)
                total = total + jnp.sum(p, axis=0, keepdims=True)
                s_buf[part, :] = p
                p_buf[part, :] = p.astype(BF16)
            inverse = 1.0 / total
            window = pl.ds(start, WIN)
            attended = (dot(v_t[:, window], p_buf[...]) * inverse).astype(BF16)
            out_grad_t = (out_grad.astype(F32).T * inverse).astype(BF16)
            delta = jnp.sum(out_grad_t.astype(F32) * attended.astype(F32), axis=0, keepdims=True)
            for c in range(WIN // KC):
                part = slice(c * KC, (c + 1) * KC)
                keys = pl.ds(pl.multiple_of(start + c * KC, 128), KC)
                dp = dot(v_all[keys, :], out_grad_t)
                ds = (s_buf[part, :] * (dp - delta)).astype(BF16)
                ds_buf[part, :] = ds
                dv_acc[a, keys, :] += dot_nt(p_buf[part, :], out_grad_t)
                dk_acc[a, keys, :] += dot(ds, q)
            dq = dot(k_t[:, window], ds_buf[...]) * scaling
            rsend[a, pl.ds(first, QT), :HS] = attended.astype(F32).T.astype(BF16)
            rsend[a, pl.ds(first, QT), HS : 2 * HS] = dq.T.astype(BF16)

        dsend[a, :, :HS] = (dk_acc[a, :SPAN, :] * scaling).astype(BF16)
        dsend[a, :, HS:] = dv_acc[a, :SPAN, :].astype(BF16)
        d_copy(a).start()

    def finish(a):
        d_copy(a).wait_recv()
        dk = dk_acc[a, SPAN:, :] * scaling + drecv[a, :, :HS].astype(F32)
        dv = dv_acc[a, SPAN:, :] + drecv[a, :, HS:].astype(F32)
        rsend[a, :, 2 * HS : 3 * HS] = dk.astype(BF16)
        rsend[a, :, 3 * HS :] = dv.astype(BF16)

    take_head(0)
    doc_shift.wait_recv()

    @pl.loop(0, OWN)
    def _(a):
        @pl.when(a < OWN - 1)
        def _():
            take_head(a + 1)

        kv_copy(a).wait_recv()
        attention(a)

        @pl.when(a > 0)
        def _():
            finish(a - 1)

            @pl.loop(1, PEERS)
            def _(d):
                ret_copy(a - 1, d).start()

            rrecv[a - 1, block(me), :] = rsend[a - 1, block(me), :]

    finish(OWN - 1)

    @pl.loop(1, PEERS)
    def _(d):
        last_copy(d).start()

    own_last = pltpu.make_async_copy(
        rsend.at[OWN - 1, block(me)], last_out.at[block(me)], out_sem.at[3]
    )
    own_last.start()

    @pl.loop(0, OWN - 1)
    def _(a):
        @pl.loop(1, PEERS)
        def _(d):
            ret_copy(a, d).wait_recv()

        @pl.loop(0, routes // 256)
        def _(c):
            rows = pl.ds(pl.multiple_of(c * 256, 256), 256)
            more = dot(slot_rows(dest_ref[rows, :], a), rrecv[a])

            @pl.when(a == 0)
            def _():
                out_acc[rows, :] = more.astype(BF16)

            @pl.when(a > 0)
            def _():
                out_acc[rows, :] = (out_acc[rows, :].astype(F32) + more).astype(BF16)

    routes_copy = pltpu.make_async_copy(out_acc, routes_out, out_sem.at[2])
    routes_copy.start()

    @pl.loop(1, PEERS)
    def _(d):
        doc_copy(d).wait_send()

    doc_shift.wait_send()

    @pl.loop(0, OWN)
    def _(a):
        @pl.loop(1, PEERS)
        def _(d):
            fwd_copy(a, d).wait_send()

        kv_copy(a).wait_send()
        d_copy(a).wait_send()

    @pl.loop(0, OWN - 1)
    def _(a):
        @pl.loop(1, PEERS)
        def _(d):
            ret_copy(a, d).wait_send()

    dest_copy.wait()
    gate_copy.wait()
    routes_copy.wait()
    own_last.wait()

    @pl.loop(1, PEERS)
    def _(d):
        last_copy(d).wait()


def home_kernel(
    routes_ref,
    last_ref,
    dest_ref,
    gate_ref,
    cot_ref,
    logits_ref,
    head_out_hbm,
    proj_out_hbm,
    grad_out,
    out_head,
    out_proj,
    out_sem,
):
    tokens = logits_ref.shape[1]
    lane = lax.broadcasted_iota(jnp.int32, (8, HS), 1)
    eye = one_hot(lax.broadcasted_iota(jnp.int32, (8, HS), 0) == lane)
    grads = jnp.zeros((8, tokens), F32)
    copies = []
    for c in range(routes_ref.shape[0] // 256):
        rows = pl.ds(c * 256, 256)
        more = dot(slot_rows(dest_ref[rows, :], OWN - 1), last_ref[...])
        full = routes_ref[rows, :].astype(F32) + more
        out_proj[rows, :] = full[:, HS:].astype(BF16)
        attended = full[:, :HS]
        out_head[rows, :] = (attended * gate_ref[rows, :]).astype(BF16)
        for n, (source, target) in enumerate(((out_head, head_out_hbm), (out_proj, proj_out_hbm))):
            copies.append(pltpu.make_async_copy(source.at[rows], target.at[rows], out_sem.at[c, n]))
            copies[-1].start()
        inner = jnp.sum(cot_ref[rows, :].astype(F32) * attended, axis=1, keepdims=True)
        r = lax.broadcasted_iota(jnp.int32, (256, HS), 0)
        lane = lax.broadcasted_iota(jnp.int32, (256, HS), 1)
        dots = jnp.where((r & 7) == lane, inner, 0.0)
        by_route = sum(dot_nt(eye, part.astype(BF16)) for part in thirds(dots))
        hot = token_rows(c, tokens)
        grads = grads + sum(dot(part.astype(BF16), hot) for part in thirds(by_route))
    gate = 1.0 / (1.0 + jnp.exp(-logits_ref[...]))
    grad_out[...] = grads * gate * (1.0 - gate)
    for copy in copies:
        copy.wait()


def per_device(projections, routed_heads, slot_index, gate_logits, doc_lengths, cotangent):
    tokens, top, width = projections.shape
    routes = tokens * top
    dma = pltpu.SemaphoreType.DMA
    vmem = pltpu.VMEM
    whole = pl.BlockSpec(memory_space=pltpu.VMEM)
    away = pl.BlockSpec(memory_space=pl.ANY)
    hbm = pl.BlockSpec(memory_space=pltpu.HBM)
    cot_rows = cotangent.reshape(routes, HS)
    logits = gate_logits.T
    handed = pl.pallas_call(
        kernel,
        out_shape=(
            jax.ShapeDtypeStruct((routes, WIDE), BF16),
            jax.ShapeDtypeStruct((SPAN, WIDE), BF16),
            jax.ShapeDtypeStruct((routes, HS), F32),
            jax.ShapeDtypeStruct((routes, HS), F32),
        ),
        in_specs=[hbm, hbm, whole, whole, whole, hbm],
        out_specs=(away, away, away, away),
        scratch_shapes=[
            pltpu.SMEM(doc_lengths.shape, jnp.int32),
            vmem((routes, 3 * HS), BF16),
            vmem((routes, HS), BF16),
            vmem((routes, HS), BF16),
            vmem((routes, HS), F32),
            vmem((routes, HS), F32),
            vmem((8, routes), F32),
            vmem((routes, WIDE), BF16),
            vmem((OWN, SPAN, WIDE), BF16),
            vmem((OWN, SPAN, WIDE), BF16),
            vmem((PEERS * 16, 128), BF16),
            vmem((PEERS * 16, 128), BF16),
            vmem((PEERS * 16, 128), BF16),
            vmem((OWN, SPAN, 2 * HS), BF16),
            vmem((OWN, SPAN, 2 * HS), BF16),
            vmem((OWN, SPAN, 2 * HS), BF16),
            vmem((OWN, SPAN, WIDE), BF16),
            vmem((OWN, SPAN, WIDE), BF16),
            vmem((2 * SPAN, HS), BF16),
            vmem((2 * SPAN, HS), BF16),
            vmem((HS, 2 * SPAN), BF16),
            vmem((HS, 2 * SPAN), BF16),
            vmem((2 * SPAN, HS), F32),
            vmem((8, SPAN), F32),
            vmem((WIN, QT), F32),
            vmem((WIN, QT), BF16),
            vmem((WIN, QT), BF16),
            vmem((OWN, 2 * SPAN, HS), F32),
            vmem((OWN, 2 * SPAN, HS), F32),
            dma((OWN, PEERS)),
            dma((OWN, PEERS)),
            dma((PEERS,)),
            dma((PEERS,)),
            dma((2,)),
            dma((OWN,)),
            dma((OWN,)),
            dma((OWN,)),
            dma((OWN,)),
            dma((OWN, PEERS)),
            dma((OWN, PEERS)),
            dma((3,)),
            dma((4,)),
        ],
        compiler_params=pltpu.CompilerParams(
            collective_id=0, has_side_effects=True, vmem_limit_bytes=44000 * 1024
        ),
    )(
        *(
            pltpu.with_memory_space_constraint(v, pltpu.HBM)
            for v in (
                projections.reshape(routes, width),
                cot_rows,
                routed_heads.T,
                slot_index.T,
                logits,
                doc_lengths,
            )
        ),
    )
    head_outputs, projection_grads, gate_grads = pl.pallas_call(
        home_kernel,
        out_shape=(
            jax.ShapeDtypeStruct((routes, HS), BF16),
            jax.ShapeDtypeStruct((routes, 3 * HS), BF16),
            jax.ShapeDtypeStruct((top, tokens), F32),
        ),
        in_specs=[whole] * 6,
        out_specs=(hbm, hbm, whole),
        scratch_shapes=[
            vmem((routes, HS), BF16),
            vmem((routes, 3 * HS), BF16),
            dma((routes // 256, 2)),
        ],
        compiler_params=pltpu.CompilerParams(vmem_limit_bytes=16000 * 1024),
    )(*handed, cot_rows, logits)
    return (
        head_outputs.reshape(tokens, top, HS),
        projection_grads.reshape(tokens, top, width),
        gate_grads.T,
    )


def solution(mesh):
    tokens = P(("seq", "head"), None, None)
    routes = P(("seq", "head"), None)
    return jax.shard_map(
        per_device,
        mesh=mesh,
        in_specs=(tokens, routes, routes, routes, P(), tokens),
        out_specs=(tokens, tokens, routes),
        check_vma=False,
    )
```

profile of v0, /device:TPU:1, one launch (start us, length us, event | category | flops | bytes accessed | tf_op | source)
XLA Modules:
  0.0 92.6 jit_solution(1985334072935859498)
XLA Ops:
  0.6 0.0 copy-start
  0.6 0.0 copy-start.1
  0.7 87.4 %shard_map.85 = (bf16[1536,512]{1,0:T(8,128)(2,1)S(1)}, bf16[768,512]{1,0:T(8,128)(2,1)S(1)}, f32[1536,128]{1,0:T(8,128)S(1)}, f32[1536,128]{1,0:T(8,128)S(1)}) custom-call(bf16[1536,384]{1,0:T(8,128)(2,1)} %bitcast.12, bf16[1536,128]{1,0:T(8,128)(2,1)} %bitcast.8, s32[8,192]{1,0:T(8,128)} %bitcast.13, s32[8,192]{1,0:T(8,128)} %bitcast.14, ...), custom_call_target="tpu_custom_call" | custom-call | tf_op jit(solution)/shard_map/pallas_call | solution.py:548
  88.1 0.0 copy-done
  88.1 0.0 copy-done.1
  88.1 4.5 %shard_map.86 = (bf16[1536,128]{1,0:T(8,128)(2,1)}, bf16[1536,384]{1,0:T(8,128)(2,1)}, f32[8,192]{1,0:T(8,128)}) custom-call(bf16[1536,512]{1,0:T(8,128)(2,1)S(1)} %get-tuple-element.10.routes_ref, bf16[768,512]{1,0:T(8,128)(2,1)S(1)} %get-tuple-element.11.last_ref, f32[1536,128]{1,0:T(8,128)S(1)} %get-tuple-element.12.dest_ref, ...), custom_call_target="tpu_custom_call" | custom-call | tf_op jit(solution)/shard_map/pallas_call | solution.py:618
Async XLA Ops:
  0.6 87.5 %copy-start = (bf16[192,8,128]{2,1,0:T(8,128)(2,1)S(1)}, bf16[192,8,128]{2,1,0:T(8,128)(2,1)}, u32[]{:S(2)}) copy-start(bf16[192,8,128]{2,1,0:T(8,128)(2,1)} %param.11) | copy-start | bytes 1179652
  0.6 87.5 %copy-start.1 = (f32[192,8]{0,1:T(8,128)S(1)}, f32[192,8]{0,1:T(8,128)}, u32[]{:S(2)}) copy-start(f32[192,8]{0,1:T(8,128)} %param.9) | copy-start | bytes 18436
where the time goes:
time: 92.8 us; the launch traced here: 92.6 us
  Pallas kernels  92 us (99%)
    pallas_call x1, Pallas kernels, per_device(): pl.pallas_call(kernel, out_shape=(jax.ShapeDtypeStruct((routes, WIDE), BF...  87.4 us
    pallas_call x1, Pallas kernels, per_device(): pl.pallas_call(home_kernel, out_shape=(jax.ShapeDtypeStruct((routes, HS),...  4.52 us

commit v1 on v0

--- a/solution.py
+++ b/solution.py
@@ -17,6 +17,8 @@
 QT = 256
 WIN = 1152
 KC = 384
+EARLY = 512
+READY = 11
 MASKED = -1e30
 F32 = jnp.float32
 BF16 = jnp.bfloat16
@@ -55,11 +57,23 @@
     return one_hot((r >> 3) + c * 32 == t)
 
 
-def slot_rows(dest, a):
+def head_slots(a):
     lane = lax.broadcasted_iota(jnp.int32, (8, SPAN), 1)
     source = div48(lane)
-    ids = (source * (OWN * CAP) + (lane - source * CAP) + a * CAP).astype(F32)
-    return one_hot(jnp.concatenate([dest] * (SPAN // 128), axis=1) == ids[0:1, :])
+    return (source * (OWN * CAP) + (lane - source * CAP) + a * CAP).astype(F32)
+
+
+def last_slots(me, start, length):
+    lane = lax.broadcasted_iota(jnp.int32, (8, length), 1) + start
+    d = div48(lane)
+    owner_x = (lax.rem(me, 4) + 4 - (d & 3)) & 3
+    owner_y = (me // 4 + 4 - (d >> 2)) & 3
+    owner = owner_y * 4 + owner_x
+    return (owner * (OWN * CAP) + (lane - d * CAP) + (OWN - 1) * CAP).astype(F32)
+
+
+def chosen(dest, ids):
+    return one_hot(jnp.concatenate([dest] * (ids.shape[1] // 128), axis=1) == ids[0:1, :])
 
 
 def kernel(
@@ -69,18 +83,15 @@
     slots_ref,
     logits_ref,
     lengths_hbm,
-    routes_out,
+    out_acc,
     last_out,
-    dest_out,
-    gate_out,
+    dest_ref,
+    gate_ref,
     lengths_ref,
     x_proj,
     x_cot,
     x_grad,
-    dest_ref,
-    gate_ref,
     rows_ref,
-    out_acc,
     fsend,
     frecv,
     doc_send,
@@ -114,7 +125,6 @@
     r_ssem,
     r_rsem,
     in_sem,
-    out_sem,
 ):
     me = lax.axis_index("head")
     here = lax.axis_index("seq")
@@ -174,7 +184,7 @@
         peer = peer_of(d)
         return pltpu.make_async_remote_copy(
             src_ref=rsend.at[OWN - 1, block(peer)],
-            dst_ref=last_out.at[block(me)],
+            dst_ref=last_out.at[block(d)],
             send_sem=r_ssem.at[OWN - 1, d],
             recv_sem=r_rsem.at[OWN - 1, d],
             device_id={"head": peer},
@@ -253,10 +263,6 @@
         x_grad[rows, :] = (x_cot[rows, :].astype(F32) * gate_ref[rows, :]).astype(BF16)
 
     proj_in.wait()
-    dest_copy = pltpu.make_async_copy(dest_ref, dest_out, out_sem.at[0])
-    gate_copy = pltpu.make_async_copy(gate_ref, gate_out, out_sem.at[1])
-    dest_copy.start()
-    gate_copy.start()
 
     def dispatch(a, c):
         first = pl.multiple_of(lax.rem(me // 4 + c, 4) * (4 * CAP), 4 * CAP)
@@ -269,6 +275,10 @@
         fsend[a, rows, 3 * HS :] = dot(hot, x_grad[...]).astype(BF16)
 
     def ship(a, c):
+        @pl.when(c == 0)
+        def _():
+            frecv[a, block(me), :] = fsend[a, block(me), :]
+
         @pl.loop(0, 4)
         def _(x):
             @pl.when(c * 4 + x > 0)
@@ -306,27 +316,26 @@
     def _(d):
         doc_copy(d).start()
 
-    @pl.loop(4, 4 * OWN)
-    def _(n):
-        dispatch(n >> 2, n & 3)
-        ship(n >> 2, n & 3)
-
-    @pl.loop(0, OWN)
-    def _(a):
-        frecv[a, block(me), :] = fsend[a, block(me), :]
-
-    @pl.loop(1, PEERS)
-    def _(d):
-        doc_copy(d).wait_recv()
-
-    doc_shift.start()
-
     def take_head(a):
         @pl.loop(1, PEERS)
         def _(d):
             fwd_copy(a, d).wait_recv()
 
         kv_copy(a).start()
+
+    @pl.loop(4, 4 * OWN)
+    def _(n):
+        @pl.when(n == 4 * OWN - 4)
+        def _():
+            @pl.loop(1, PEERS)
+            def _(d):
+                doc_copy(d).wait_recv()
+
+            doc_shift.start()
+            take_head(0)
+
+        dispatch(n >> 2, n & 3)
+        ship(n >> 2, n & 3)
 
     def head_docs(a, docs_ref):
         r = lax.broadcasted_iota(jnp.int32, (SPAN, 128), 0)
@@ -407,7 +416,6 @@
         rsend[a, :, 2 * HS : 3 * HS] = dk.astype(BF16)
         rsend[a, :, 3 * HS :] = dv.astype(BF16)
 
-    take_head(0)
     doc_shift.wait_recv()
 
     @pl.loop(0, OWN)
@@ -435,10 +443,7 @@
     def _(d):
         last_copy(d).start()
 
-    own_last = pltpu.make_async_copy(
-        rsend.at[OWN - 1, block(me)], last_out.at[block(me)], out_sem.at[3]
-    )
-    own_last.start()
+    last_out[:CAP, :] = rsend[OWN - 1, block(me), :]
 
     @pl.loop(0, OWN - 1)
     def _(a):
@@ -449,7 +454,7 @@
         @pl.loop(0, routes // 256)
         def _(c):
             rows = pl.ds(pl.multiple_of(c * 256, 256), 256)
-            more = dot(slot_rows(dest_ref[rows, :], a), rrecv[a])
+            more = dot(chosen(dest_ref[rows, :], head_slots(a)), rrecv[a])
 
             @pl.when(a == 0)
             def _():
@@ -459,8 +464,17 @@
             def _():
                 out_acc[rows, :] = (out_acc[rows, :].astype(F32) + more).astype(BF16)
 
-    routes_copy = pltpu.make_async_copy(out_acc, routes_out, out_sem.at[2])
-    routes_copy.start()
+    @pl.loop(1, READY)
+    def _(d):
+        last_copy(d).wait_recv()
+
+    early = last_slots(me, 0, EARLY)
+
+    @pl.loop(0, routes // 256)
+    def _(c):
+        rows = pl.ds(pl.multiple_of(c * 256, 256), 256)
+        more = dot(chosen(dest_ref[rows, :], early), last_out[:EARLY, :])
+        out_acc[rows, :] = (out_acc[rows, :].astype(F32) + more).astype(BF16)
 
     @pl.loop(1, PEERS)
     def _(d):
@@ -483,14 +497,13 @@
         def _(d):
             ret_copy(a, d).wait_send()
 
-    dest_copy.wait()
-    gate_copy.wait()
-    routes_copy.wait()
-    own_last.wait()
-
     @pl.loop(1, PEERS)
     def _(d):
-        last_copy(d).wait()
+        last_copy(d).wait_send()
+
+    @pl.loop(READY, PEERS)
+    def _(d):
+        last_copy(d).wait_recv()
 
 
 def home_kernel(
@@ -508,13 +521,14 @@
     out_sem,
 ):
     tokens = logits_ref.shape[1]
+    late = last_slots(lax.axis_index("head"), EARLY, SPAN - EARLY)
     lane = lax.broadcasted_iota(jnp.int32, (8, HS), 1)
     eye = one_hot(lax.broadcasted_iota(jnp.int32, (8, HS), 0) == lane)
     grads = jnp.zeros((8, tokens), F32)
     copies = []
     for c in range(routes_ref.shape[0] // 256):
         rows = pl.ds(c * 256, 256)
-        more = dot(slot_rows(dest_ref[rows, :], OWN - 1), last_ref[...])
+        more = dot(chosen(dest_ref[rows, :], late), last_ref[EARLY:, :])
         full = routes_ref[rows, :].astype(F32) + more
         out_proj[rows, :] = full[:, HS:].astype(BF16)
         attended = full[:, :HS]
@@ -541,7 +555,6 @@
     dma = pltpu.SemaphoreType.DMA
     vmem = pltpu.VMEM
     whole = pl.BlockSpec(memory_space=pltpu.VMEM)
-    away = pl.BlockSpec(memory_space=pl.ANY)
     hbm = pl.BlockSpec(memory_space=pltpu.HBM)
     cot_rows = cotangent.reshape(routes, HS)
     logits = gate_logits.T
@@ -554,16 +567,13 @@
             jax.ShapeDtypeStruct((routes, HS), F32),
         ),
         in_specs=[hbm, hbm, whole, whole, whole, hbm],
-        out_specs=(away, away, away, away),
+        out_specs=(whole, whole, whole, whole),
         scratch_shapes=[
             pltpu.SMEM(doc_lengths.shape, jnp.int32),
             vmem((routes, 3 * HS), BF16),
             vmem((routes, HS), BF16),
             vmem((routes, HS), BF16),
-            vmem((routes, HS), F32),
-            vmem((routes, HS), F32),
             vmem((8, routes), F32),
-            vmem((routes, WIDE), BF16),
             vmem((OWN, SPAN, WIDE), BF16),
             vmem((OWN, SPAN, WIDE), BF16),
             vmem((PEERS * 16, 128), BF16),
@@ -597,7 +607,6 @@
             dma((OWN, PEERS)),
             dma((OWN, PEERS)),
             dma((3,)),
-            dma((4,)),
         ],
         compiler_params=pltpu.CompilerParams(
             collective_id=0, has_side_effects=True, vmem_limit_bytes=44000 * 1024

time: 92.8 us -> 93.4 us (level)
  the two profiles are of different devices: /device:TPU:1 before, /device:TPU:97 now
where the time goes in v1:
time: 93.4 us; the launch traced here: 92.7 us
  Pallas kernels  92.1 us (99%)
    pallas_call x1, Pallas kernels, per_device(): pl.pallas_call(kernel, out_shape=(jax.ShapeDtypeStruct((routes, WIDE), BF...  88.4 us
    pallas_call x1, Pallas kernels, per_device(): pl.pallas_call(home_kernel, out_shape=(jax.ShapeDtypeStruct((routes, HS),...  3.67 us

profile of v1, /device:TPU:97, one launch (start us, length us, event | category | flops | bytes accessed | tf_op | source)
XLA Modules:
  0.0 92.7 jit_solution(5515084963318233866)
XLA Ops:
  0.6 0.0 copy-start
  0.6 0.0 copy-start.1
  0.7 88.4 %shard_map.85 = (bf16[1536,512]{1,0:T(8,128)(2,1)S(1)}, bf16[768,512]{1,0:T(8,128)(2,1)S(1)}, f32[1536,128]{1,0:T(8,128)S(1)}, f32[1536,128]{1,0:T(8,128)S(1)}) custom-call(bf16[1536,384]{1,0:T(8,128)(2,1)} %bitcast.12, bf16[1536,128]{1,0:T(8,128)(2,1)} %bitcast.8, s32[8,192]{1,0:T(8,128)} %bitcast.13, s32[8,192]{1,0:T(8,128)} %bitcast.14, ...), custom_call_target="tpu_custom_call" | custom-call | tf_op jit(solution)/shard_map/pallas_call | solution.py:561
  89.0 0.0 copy-done
  89.1 0.0 copy-done.1
  89.1 3.7 %shard_map.86 = (bf16[1536,128]{1,0:T(8,128)(2,1)}, bf16[1536,384]{1,0:T(8,128)(2,1)}, f32[8,192]{1,0:T(8,128)}) custom-call(bf16[1536,512]{1,0:T(8,128)(2,1)S(1)} %get-tuple-element.10.routes_ref, bf16[768,512]{1,0:T(8,128)(2,1)S(1)} %get-tuple-element.11.last_ref, f32[1536,128]{1,0:T(8,128)S(1)} %get-tuple-element.12.dest_ref, ...), custom_call_target="tpu_custom_call" | custom-call | tf_op jit(solution)/shard_map/pallas_call | solution.py:627
Async XLA Ops:
  0.6 88.4 %copy-start = (bf16[192,8,128]{2,1,0:T(8,128)(2,1)S(1)}, bf16[192,8,128]{2,1,0:T(8,128)(2,1)}, u32[]{:S(2)}) copy-start(bf16[192,8,128]{2,1,0:T(8,128)(2,1)} %param.11) | copy-start | bytes 1179652
  0.6 88.4 %copy-start.1 = (f32[192,8]{0,1:T(8,128)S(1)}, f32[192,8]{0,1:T(8,128)}, u32[]{:S(2)}) copy-start(f32[192,8]{0,1:T(8,128)} %param.9) | copy-start | bytes 18436

commit v2 on v1

--- a/solution.py
+++ b/solution.py
@@ -17,8 +17,6 @@
 QT = 256
 WIN = 1152
 KC = 384
-EARLY = 512
-READY = 11
 MASKED = -1e30
 F32 = jnp.float32
 BF16 = jnp.bfloat16
@@ -61,15 +59,6 @@
     lane = lax.broadcasted_iota(jnp.int32, (8, SPAN), 1)
     source = div48(lane)
     return (source * (OWN * CAP) + (lane - source * CAP) + a * CAP).astype(F32)
-
-
-def last_slots(me, start, length):
-    lane = lax.broadcasted_iota(jnp.int32, (8, length), 1) + start
-    d = div48(lane)
-    owner_x = (lax.rem(me, 4) + 4 - (d & 3)) & 3
-    owner_y = (me // 4 + 4 - (d >> 2)) & 3
-    owner = owner_y * 4 + owner_x
-    return (owner * (OWN * CAP) + (lane - d * CAP) + (OWN - 1) * CAP).astype(F32)
 
 
 def chosen(dest, ids):
@@ -84,7 +73,7 @@
     logits_ref,
     lengths_hbm,
     out_acc,
-    last_out,
+    rrecv,
     dest_ref,
     gate_ref,
     lengths_ref,
@@ -101,7 +90,6 @@
     dsend,
     drecv,
     rsend,
-    rrecv,
     k_all,
     v_all,
     k_t,
@@ -169,27 +157,23 @@
             device_id_type=MESH,
         )
 
-    def ret_copy(a, d):
+    def ret_copy(a, half, d):
         peer = peer_of(d)
         return pltpu.make_async_remote_copy(
-            src_ref=rsend.at[a, block(peer)],
-            dst_ref=rrecv.at[a, block(me)],
-            send_sem=r_ssem.at[a, d],
-            recv_sem=r_rsem.at[a, d],
+            src_ref=rsend.at[a, half, block(peer)],
+            dst_ref=rrecv.at[a, half, block(me)],
+            send_sem=r_ssem.at[a, half, d],
+            recv_sem=r_rsem.at[a, half, d],
             device_id={"head": peer},
             device_id_type=MESH,
         )
 
-    def last_copy(d):
-        peer = peer_of(d)
-        return pltpu.make_async_remote_copy(
-            src_ref=rsend.at[OWN - 1, block(peer)],
-            dst_ref=last_out.at[block(d)],
-            send_sem=r_ssem.at[OWN - 1, d],
-            recv_sem=r_rsem.at[OWN - 1, d],
-            device_id={"head": peer},
-            device_id_type=MESH,
-        )
+    def send_home(a, half):
+        @pl.loop(1, PEERS)
+        def _(d):
+            ret_copy(a, half, d).start()
+
+        rrecv[a, half, block(me), :] = rsend[a, half, block(me), :]
 
     def doc_rows(i):
         return pl.ds(pl.multiple_of(i * 16, 16), 16)
@@ -325,17 +309,15 @@
 
     @pl.loop(4, 4 * OWN)
     def _(n):
-        @pl.when(n == 4 * OWN - 4)
-        def _():
-            @pl.loop(1, PEERS)
-            def _(d):
-                doc_copy(d).wait_recv()
-
-            doc_shift.start()
-            take_head(0)
-
         dispatch(n >> 2, n & 3)
         ship(n >> 2, n & 3)
+
+    @pl.loop(1, PEERS)
+    def _(d):
+        doc_copy(d).wait_recv()
+
+    doc_shift.start()
+    take_head(0)
 
     def head_docs(a, docs_ref):
         r = lax.broadcasted_iota(jnp.int32, (SPAN, 128), 0)
@@ -345,6 +327,14 @@
         pick = one_hot(jnp.concatenate([lane, lane + 128], axis=1) == jnp.concatenate([wanted] * 2, axis=1))
         spread = dot(pick, docs_ref[...])
         return jnp.where(lane == r - source * CAP, spread, 0.0).astype(BF16)
+
+    def finish(a):
+        d_copy(a).wait_recv()
+        dk = dk_acc[a, SPAN:, :] * scaling + drecv[a, :, :HS].astype(F32)
+        dv = dv_acc[a, SPAN:, :] + drecv[a, :, HS:].astype(F32)
+        rsend[a, 1, :, :HS] = dk.astype(BF16)
+        rsend[a, 1, :, HS:] = dv.astype(BF16)
+        send_home(a, 1)
 
     def attention(a):
         k_all[:SPAN, :] = kv_prev[a, :, :HS]
@@ -363,6 +353,14 @@
 
         @pl.loop(0, SPAN // QT)
         def _(i):
+            @pl.when((i == 1) & (a < OWN - 1))
+            def _():
+                take_head(a + 1)
+
+            @pl.when((i == 2) & (a > 0))
+            def _():
+                finish(a - 1)
+
             first = pl.multiple_of(i * QT, QT)
             start = pl.multiple_of(((i * (i + 1)) >> 1) * 128, 128)
             q = frecv[a, pl.ds(first, QT), :HS]
@@ -402,59 +400,38 @@
                 dv_acc[a, keys, :] += dot_nt(p_buf[part, :], out_grad_t)
                 dk_acc[a, keys, :] += dot(ds, q)
             dq = dot(k_t[:, window], ds_buf[...]) * scaling
-            rsend[a, pl.ds(first, QT), :HS] = attended.astype(F32).T.astype(BF16)
-            rsend[a, pl.ds(first, QT), HS : 2 * HS] = dq.T.astype(BF16)
+            rsend[a, 0, pl.ds(first, QT), :HS] = attended.astype(F32).T.astype(BF16)
+            rsend[a, 0, pl.ds(first, QT), HS:] = dq.T.astype(BF16)
 
         dsend[a, :, :HS] = (dk_acc[a, :SPAN, :] * scaling).astype(BF16)
         dsend[a, :, HS:] = dv_acc[a, :SPAN, :].astype(BF16)
         d_copy(a).start()
-
-    def finish(a):
-        d_copy(a).wait_recv()
-        dk = dk_acc[a, SPAN:, :] * scaling + drecv[a, :, :HS].astype(F32)
-        dv = dv_acc[a, SPAN:, :] + drecv[a, :, HS:].astype(F32)
-        rsend[a, :, 2 * HS : 3 * HS] = dk.astype(BF16)
-        rsend[a, :, 3 * HS :] = dv.astype(BF16)
+        send_home(a, 0)
 
     doc_shift.wait_recv()
 
     @pl.loop(0, OWN)
     def _(a):
-        @pl.when(a < OWN - 1)
-        def _():
-            take_head(a + 1)
-
         kv_copy(a).wait_recv()
         attention(a)
 
-        @pl.when(a > 0)
-        def _():
-            finish(a - 1)
-
-            @pl.loop(1, PEERS)
-            def _(d):
-                ret_copy(a - 1, d).start()
-
-            rrecv[a - 1, block(me), :] = rsend[a - 1, block(me), :]
-
     finish(OWN - 1)
 
-    @pl.loop(1, PEERS)
-    def _(d):
-        last_copy(d).start()
-
-    last_out[:CAP, :] = rsend[OWN - 1, block(me), :]
+    def await_home(a):
+        @pl.loop(1, PEERS)
+        def _(d):
+            ret_copy(a, 0, d).wait_recv()
+            ret_copy(a, 1, d).wait_recv()
 
     @pl.loop(0, OWN - 1)
     def _(a):
-        @pl.loop(1, PEERS)
-        def _(d):
-            ret_copy(a, d).wait_recv()
+        await_home(a)
 
         @pl.loop(0, routes // 256)
         def _(c):
             rows = pl.ds(pl.multiple_of(c * 256, 256), 256)
-            more = dot(chosen(dest_ref[rows, :], head_slots(a)), rrecv[a])
+            hot = chosen(dest_ref[rows, :], head_slots(a))
+            more = jnp.concatenate([dot(hot, rrecv[a, 0]), dot(hot, rrecv[a, 1])], axis=1)
 
             @pl.when(a == 0)
             def _():
@@ -463,18 +440,6 @@
             @pl.when(a > 0)
             def _():
                 out_acc[rows, :] = (out_acc[rows, :].astype(F32) + more).astype(BF16)
-
-    @pl.loop(1, READY)
-    def _(d):
-        last_copy(d).wait_recv()
-
-    early = last_slots(me, 0, EARLY)
-
-    @pl.loop(0, routes // 256)
-    def _(c):
-        rows = pl.ds(pl.multiple_of(c * 256, 256), 256)
-        more = dot(chosen(dest_ref[rows, :], early), last_out[:EARLY, :])
-        out_acc[rows, :] = (out_acc[rows, :].astype(F32) + more).astype(BF16)
 
     @pl.loop(1, PEERS)
     def _(d):
@@ -491,19 +456,14 @@
         kv_copy(a).wait_send()
         d_copy(a).wait_send()
 
-    @pl.loop(0, OWN - 1)
+    @pl.loop(0, OWN)
     def _(a):
         @pl.loop(1, PEERS)
         def _(d):
-            ret_copy(a, d).wait_send()
-
-    @pl.loop(1, PEERS)
-    def _(d):
-        last_copy(d).wait_send()
-
-    @pl.loop(READY, PEERS)
-    def _(d):
-        last_copy(d).wait_recv()
+            ret_copy(a, 0, d).wait_send()
+            ret_copy(a, 1, d).wait_send()
+
+    await_home(OWN - 1)
 
 
 def home_kernel(
@@ -521,16 +481,18 @@
     out_sem,
 ):
     tokens = logits_ref.shape[1]
-    late = last_slots(lax.axis_index("head"), EARLY, SPAN - EARLY)
+    late = head_slots(OWN - 1)
     lane = lax.broadcasted_iota(jnp.int32, (8, HS), 1)
     eye = one_hot(lax.broadcasted_iota(jnp.int32, (8, HS), 0) == lane)
     grads = jnp.zeros((8, tokens), F32)
     copies = []
     for c in range(routes_ref.shape[0] // 256):
         rows = pl.ds(c * 256, 256)
-        more = dot(chosen(dest_ref[rows, :], late), last_ref[EARLY:, :])
-        full = routes_ref[rows, :].astype(F32) + more
-        out_proj[rows, :] = full[:, HS:].astype(BF16)
+        hot = chosen(dest_ref[rows, :], late)
+        full = routes_ref[rows, : 2 * HS].astype(F32) + dot(hot, last_ref[OWN - 1, 0])
+        rest = routes_ref[rows, 2 * HS :].astype(F32) + dot(hot, last_ref[OWN - 1, 1])
+        out_proj[rows, :HS] = full[:, HS:].astype(BF16)
+        out_proj[rows, HS:] = rest.astype(BF16)
         attended = full[:, :HS]
         out_head[rows, :] = (attended * gate_ref[rows, :]).astype(BF16)
         for n, (source, target) in enumerate(((out_head, head_out_hbm), (out_proj, proj_out_hbm))):
@@ -562,7 +524,7 @@
         kernel,
         out_shape=(
             jax.ShapeDtypeStruct((routes, WIDE), BF16),
-            jax.ShapeDtypeStruct((SPAN, WIDE), BF16),
+            jax.ShapeDtypeStruct((OWN, 2, SPAN, 2 * HS), BF16),
             jax.ShapeDtypeStruct((routes, HS), F32),
             jax.ShapeDtypeStruct((routes, HS), F32),
         ),
@@ -582,8 +544,7 @@
             vmem((OWN, SPAN, 2 * HS), BF16),
             vmem((OWN, SPAN, 2 * HS), BF16),
             vmem((OWN, SPAN, 2 * HS), BF16),
-            vmem((OWN, SPAN, WIDE), BF16),
-            vmem((OWN, SPAN, WIDE), BF16),
+            vmem((OWN, 2, SPAN, 2 * HS), BF16),
             vmem((2 * SPAN, HS), BF16),
             vmem((2 * SPAN, HS), BF16),
             vmem((HS, 2 * SPAN), BF16),
@@ -604,8 +565,8 @@
             dma((OWN,)),
             dma((OWN,)),
             dma((OWN,)),
-            dma((OWN, PEERS)),
-            dma((OWN, PEERS)),
+            dma((OWN, 2, PEERS)),
+            dma((OWN, 2, PEERS)),
             dma((3,)),
         ],
         compiler_params=pltpu.CompilerParams(

time: 93.4 us -> 89.1 us (0.954)
  Pallas kernels: 92.1 us -> 88.1 us
    pallas_call x1, Pallas kernels: 88.4 us -> 83.6 us  [per_device(): pl.pallas_call(kernel, out_shape=(jax.ShapeDtypeStruct((routes, WIDE), BF...]
where the time goes in v2:
time: 89.1 us; the launch traced here: 88.8 us
  Pallas kernels  88.1 us (99%)
    pallas_call x1, Pallas kernels, per_device(): pl.pallas_call(kernel, out_shape=(jax.ShapeDtypeStruct((routes, WIDE), BF...  83.6 us
    pallas_call x1, Pallas kernels, per_device(): pl.pallas_call(home_kernel, out_shape=(jax.ShapeDtypeStruct((routes, HS),...  4.48 us

profile of v2, /device:TPU:97, one launch (start us, length us, event | category | flops | bytes accessed | tf_op | source)
XLA Modules:
  0.0 88.8 jit_solution(7479454985484669144)
XLA Ops:
  0.6 0.0 copy-start
  0.6 0.0 copy-start.1
  0.7 83.6 %shard_map.85 = (bf16[1536,512]{1,0:T(8,128)(2,1)S(1)}, bf16[4,2,768,256]{3,2,1,0:T(8,128)(2,1)S(1)}, f32[1536,128]{1,0:T(8,128)S(1)}, f32[1536,128]{1,0:T(8,128)S(1)}) custom-call(bf16[1536,384]{1,0:T(8,128)(2,1)} %bitcast.12, bf16[1536,128]{1,0:T(8,128)(2,1)} %bitcast.8, s32[8,192]{1,0:T(8,128)} %bitcast.13, s32[8,192]{1,0:T(8,128)} %bitcast.14, ...), custom_call_target="tpu_custom_call" | custom-call | tf_op jit(solution)/shard_map/pallas_call | solution.py:523
  84.3 0.0 copy-done
  84.3 0.0 copy-done.1
  84.3 4.5 %shard_map.86 = (bf16[1536,128]{1,0:T(8,128)(2,1)}, bf16[1536,384]{1,0:T(8,128)(2,1)}, f32[8,192]{1,0:T(8,128)}) custom-call(bf16[1536,512]{1,0:T(8,128)(2,1)S(1)} %get-tuple-element.10.routes_ref, bf16[4,2,768,256]{3,2,1,0:T(8,128)(2,1)S(1)} %get-tuple-element.11.last_ref, f32[1536,128]{1,0:T(8,128)S(1)} %get-tuple-element.12.dest_ref, ...), custom_call_target="tpu_custom_call" | custom-call | tf_op jit(solution)/shard_map/pallas_call | solution.py:588
Async XLA Ops:
  0.6 83.7 %copy-start = (bf16[192,8,128]{2,1,0:T(8,128)(2,1)S(1)}, bf16[192,8,128]{2,1,0:T(8,128)(2,1)}, u32[]{:S(2)}) copy-start(bf16[192,8,128]{2,1,0:T(8,128)(2,1)} %param.11) | copy-start | bytes 1179652
  0.6 83.7 %copy-start.1 = (f32[192,8]{0,1:T(8,128)S(1)}, f32[192,8]{0,1:T(8,128)}, u32[]{:S(2)}) copy-start(f32[192,8]{0,1:T(8,128)} %param.9) | copy-start | bytes 18436

commit v3 on v2

--- a/solution.py
+++ b/solution.py
@@ -351,57 +351,65 @@
         dk_acc[a] = jnp.zeros((2 * SPAN, HS), F32)
         dv_acc[a] = jnp.zeros((2 * SPAN, HS), F32)
 
-        @pl.loop(0, SPAN // QT)
-        def _(i):
-            @pl.when((i == 1) & (a < OWN - 1))
-            def _():
-                take_head(a + 1)
-
-            @pl.when((i == 2) & (a > 0))
-            def _():
-                finish(a - 1)
-
-            first = pl.multiple_of(i * QT, QT)
-            start = pl.multiple_of(((i * (i + 1)) >> 1) * 128, 128)
-            q = frecv[a, pl.ds(first, QT), :HS]
-            out_grad = frecv[a, pl.ds(first, QT), 3 * HS :]
-            q_docs = query_docs[0:1, pl.ds(first, QT)]
+        for i in range(SPAN // QT):
+            if i == 1:
+
+                @pl.when(a < OWN - 1)
+                def _():
+                    take_head(a + 1)
+
+            if i == 2:
+
+                @pl.when(a > 0)
+                def _():
+                    finish(a - 1)
+
+            first = i * QT
+            left = first // CAP * CAP
+            right = SPAN + first + QT
+            start = left // 128 * 128
+            skip = left - start
+            cuts = [min(left + c * KC, right) for c in range((right - left - 1) // KC + 2)]
+            chunks = list(zip(cuts, cuts[1:]))
+            if skip:
+                p_buf[:skip, :] = jnp.zeros((skip, QT), BF16)
+                ds_buf[:skip, :] = jnp.zeros((skip, QT), BF16)
+            q = frecv[a, first : first + QT, :HS]
+            out_grad = frecv[a, first : first + QT, 3 * HS :]
+            q_docs = query_docs[0:1, first : first + QT]
             top = jnp.full((1, QT), MASKED, F32)
-            for c in range(WIN // KC):
-                keys = pl.ds(pl.multiple_of(start + c * KC, 128), KC)
-                s = dot_nt(k_all[keys, :], q) * (scaling * math.log2(math.e))
-                docs = key_docs[keys, :]
+            for low, high in chunks:
+                s = dot_nt(k_all[low:high, :], q) * (scaling * math.log2(math.e))
+                docs = key_docs[low:high, :]
                 seen = jnp.concatenate([docs, docs], axis=1) == q_docs
-                if (c + 1) * KC > SPAN:
-                    k_at = lax.broadcasted_iota(jnp.int32, (KC, QT), 0) + (start + c * KC - SPAN)
-                    q_at = lax.broadcasted_iota(jnp.int32, (KC, QT), 1) + first
+                if high > SPAN + first:
+                    k_at = lax.broadcasted_iota(jnp.int32, s.shape, 0) + (low - SPAN)
+                    q_at = lax.broadcasted_iota(jnp.int32, s.shape, 1) + first
                     seen = seen & (k_at <= q_at)
                 s = jnp.where(seen, s, MASKED)
-                s_buf[c * KC : (c + 1) * KC, :] = s
+                s_buf[low - start : high - start, :] = s
                 top = jnp.maximum(top, jnp.max(s, axis=0, keepdims=True))
             total = jnp.zeros((1, QT), F32)
-            for c in range(WIN // KC):
-                part = slice(c * KC, (c + 1) * KC)
+            for low, high in chunks:
+                part = slice(low - start, high - start)
                 p = jnp.exp2(s_buf[part, :] - top)
                 total = total + jnp.sum(p, axis=0, keepdims=True)
                 s_buf[part, :] = p
                 p_buf[part, :] = p.astype(BF16)
             inverse = 1.0 / total
-            window = pl.ds(start, WIN)
-            attended = (dot(v_t[:, window], p_buf[...]) * inverse).astype(BF16)
+            attended = (dot(v_t[:, start:right], p_buf[: right - start, :]) * inverse).astype(BF16)
             out_grad_t = (out_grad.astype(F32).T * inverse).astype(BF16)
             delta = jnp.sum(out_grad_t.astype(F32) * attended.astype(F32), axis=0, keepdims=True)
-            for c in range(WIN // KC):
-                part = slice(c * KC, (c + 1) * KC)
-                keys = pl.ds(pl.multiple_of(start + c * KC, 128), KC)
-                dp = dot(v_all[keys, :], out_grad_t)
+            for low, high in chunks:
+                part = slice(low - start, high - start)
+                dp = dot(v_all[low:high, :], out_grad_t)
                 ds = (s_buf[part, :] * (dp - delta)).astype(BF16)
                 ds_buf[part, :] = ds
-                dv_acc[a, keys, :] += dot_nt(p_buf[part, :], out_grad_t)
-                dk_acc[a, keys, :] += dot(ds, q)
-            dq = dot(k_t[:, window], ds_buf[...]) * scaling
-            rsend[a, 0, pl.ds(first, QT), :HS] = attended.astype(F32).T.astype(BF16)
-            rsend[a, 0, pl.ds(first, QT), HS:] = dq.T.astype(BF16)
+                dv_acc[a, low:high, :] += dot_nt(p_buf[part, :], out_grad_t)
+                dk_acc[a, low:high, :] += dot(ds, q)
+            dq = dot(k_t[:, start:right], ds_buf[: right - start, :]) * scaling
+            rsend[a, 0, first : first + QT, :HS] = attended.astype(F32).T.astype(BF16)
+            rsend[a, 0, first : first + QT, HS:] = dq.T.astype(BF16)
 
         dsend[a, :, :HS] = (dk_acc[a, :SPAN, :] * scaling).astype(BF16)
         dsend[a, :, HS:] = dv_acc[a, :SPAN, :].astype(BF16)
@@ -415,17 +423,14 @@
         kv_copy(a).wait_recv()
         attention(a)
 
-    finish(OWN - 1)
-
-    def await_home(a):
+    def await_half(a, half):
         @pl.loop(1, PEERS)
         def _(d):
-            ret_copy(a, 0, d).wait_recv()
-            ret_copy(a, 1, d).wait_recv()
-
-    @pl.loop(0, OWN - 1)
-    def _(a):
-        await_home(a)
+            ret_copy(a, half, d).wait_recv()
+
+    def combine(a):
+        await_half(a, 0)
+        await_half(a, 1)
 
         @pl.loop(0, routes // 256)
         def _(c):
@@ -440,6 +445,23 @@
             @pl.when(a > 0)
             def _():
                 out_acc[rows, :] = (out_acc[rows, :].astype(F32) + more).astype(BF16)
+
+    @pl.loop(0, OWN - 1)
+    def _(a):
+        @pl.when(a == OWN - 2)
+        def _():
+            finish(OWN - 1)
+
+        combine(a)
+
+    await_half(OWN - 1, 0)
+
+    @pl.loop(0, routes // 256)
+    def _(c):
+        rows = pl.ds(pl.multiple_of(c * 256, 256), 256)
+        hot = chosen(dest_ref[rows, :], head_slots(OWN - 1))
+        more = dot(hot, rrecv[OWN - 1, 0])
+        out_acc[rows, : 2 * HS] = (out_acc[rows, : 2 * HS].astype(F32) + more).astype(BF16)
 
     @pl.loop(1, PEERS)
     def _(d):
@@ -463,7 +485,7 @@
             ret_copy(a, 0, d).wait_send()
             ret_copy(a, 1, d).wait_send()
 
-    await_home(OWN - 1)
+    await_half(OWN - 1, 1)
 
 
 def home_kernel(
@@ -489,11 +511,10 @@
     for c in range(routes_ref.shape[0] // 256):
         rows = pl.ds(c * 256, 256)
         hot = chosen(dest_ref[rows, :], late)
-        full = routes_ref[rows, : 2 * HS].astype(F32) + dot(hot, last_ref[OWN - 1, 0])
         rest = routes_ref[rows, 2 * HS :].astype(F32) + dot(hot, last_ref[OWN - 1, 1])
-        out_proj[rows, :HS] = full[:, HS:].astype(BF16)
+        out_proj[rows, :HS] = routes_ref[rows, HS : 2 * HS]
         out_proj[rows, HS:] = rest.astype(BF16)
-        attended = full[:, :HS]
+        attended = routes_ref[rows, :HS].astype(F32)
         out_head[rows, :] = (attended * gate_ref[rows, :]).astype(BF16)
         for n, (source, target) in enumerate(((out_head, head_out_hbm), (out_proj, proj_out_hbm))):
             copies.append(pltpu.make_async_copy(source.at[rows], target.at[rows], out_sem.at[c, n]))

time: 89.1 us -> 89.2 us (level); the launches traced: 88.8 us -> 87.7 us
  Pallas kernels: 88.1 us -> 87 us
    pallas_call x1, Pallas kernels: 4.48 us -> 3.17 us  [per_device(): pl.pallas_call(home_kernel, out_shape=(jax.ShapeDtypeStruct((routes, HS),...]
where the time goes in v3:
time: 89.2 us; the launch traced here: 87.7 us
  Pallas kernels  87 us (98%)
    pallas_call x1, Pallas kernels, per_device(): pl.pallas_call(kernel, out_shape=(jax.ShapeDtypeStruct((routes, WIDE), BF...  83.8 us
    pallas_call x1, Pallas kernels, per_device(): pl.pallas_call(home_kernel, out_shape=(jax.ShapeDtypeStruct((routes, HS),...  3.17 us

profile of v3, /device:TPU:97, one launch (start us, length us, event | category | flops | bytes accessed | tf_op | source)
XLA Modules:
  0.0 87.7 jit_solution(9834460896876213352)
XLA Ops:
  0.6 0.0 copy-start
  0.6 0.0 copy-start.1
  0.7 83.8 %shard_map.85 = (bf16[1536,512]{1,0:T(8,128)(2,1)S(1)}, bf16[4,2,768,256]{3,2,1,0:T(8,128)(2,1)S(1)}, f32[1536,128]{1,0:T(8,128)S(1)}, f32[1536,128]{1,0:T(8,128)S(1)}) custom-call(bf16[1536,384]{1,0:T(8,128)(2,1)} %bitcast.12, bf16[1536,128]{1,0:T(8,128)(2,1)} %bitcast.8, s32[8,192]{1,0:T(8,128)} %bitcast.13, s32[8,192]{1,0:T(8,128)} %bitcast.14, ...), custom_call_target="tpu_custom_call" | custom-call | tf_op jit(solution)/shard_map/pallas_call | solution.py:544
  84.5 0.0 copy-done
  84.5 0.0 copy-done.1
  84.5 3.2 %shard_map.86 = (bf16[1536,128]{1,0:T(8,128)(2,1)}, bf16[1536,384]{1,0:T(8,128)(2,1)}, f32[8,192]{1,0:T(8,128)}) custom-call(bf16[1536,512]{1,0:T(8,128)(2,1)S(1)} %get-tuple-element.10.routes_ref, bf16[4,2,768,256]{3,2,1,0:T(8,128)(2,1)S(1)} %get-tuple-element.11.last_ref, f32[1536,128]{1,0:T(8,128)S(1)} %get-tuple-element.12.dest_ref, ...), custom_call_target="tpu_custom_call" | custom-call | tf_op jit(solution)/shard_map/pallas_call | solution.py:609
Async XLA Ops:
  0.6 83.8 %copy-start = (bf16[192,8,128]{2,1,0:T(8,128)(2,1)S(1)}, bf16[192,8,128]{2,1,0:T(8,128)(2,1)}, u32[]{:S(2)}) copy-start(bf16[192,8,128]{2,1,0:T(8,128)(2,1)} %param.11) | copy-start | bytes 1179652
  0.6 83.8 %copy-start.1 = (f32[192,8]{0,1:T(8,128)S(1)}, f32[192,8]{0,1:T(8,128)}, u32[]{:S(2)}) copy-start(f32[192,8]{0,1:T(8,128)} %param.9) | copy-start | bytes 18436

commit v4 on v3

--- a/solution.py
+++ b/solution.py
@@ -80,6 +80,7 @@
     x_proj,
     x_cot,
     x_grad,
+    mixed_ref,
     rows_ref,
     fsend,
     frecv,
@@ -116,8 +117,8 @@
 ):
     me = lax.axis_index("head")
     here = lax.axis_index("seq")
-    after = lax.rem(here + 1, PEERS)
-    before = lax.rem(here + PEERS - 1, PEERS)
+    after = (here + 1) & (PEERS - 1)
+    before = (here + PEERS - 1) & (PEERS - 1)
     routes = proj_hbm.shape[0]
     tokens = heads_ref.shape[1]
     tiles = routes // 128
@@ -132,8 +133,8 @@
     barrier = pltpu.get_barrier_semaphore()
 
     def peer_of(d):
-        px = lax.rem(lax.rem(me, 4) + lax.rem(d, 4), 4)
-        py = lax.rem(me // 4 + d // 4, 4)
+        px = (me + d) & 3
+        py = ((me >> 2) + (d >> 2)) & 3
         return py * 4 + px
 
     @pl.loop(1, PEERS)
@@ -231,8 +232,8 @@
         r = lax.broadcasted_iota(jnp.int32, (256, count), 0)
         f = lax.broadcasted_iota(jnp.int32, (256, count), 1)
         mixed = jnp.where((r & 7) == (f & 7), mixed, 0.0).astype(BF16)
+        mixed_ref[rows, :] = mixed
         f = lax.broadcasted_iota(jnp.int32, (count, 128), 0)
-        dest_ref[rows, :] = dot(mixed, dest_weight(f))
         gate_ref[rows, :] = dot(mixed, one_hot(f >= 16))
         f = lax.broadcasted_iota(jnp.int32, (8, count), 1)
         want = lax.broadcasted_iota(jnp.int32, (8, count), 0)
@@ -249,7 +250,7 @@
     proj_in.wait()
 
     def dispatch(a, c):
-        first = pl.multiple_of(lax.rem(me // 4 + c, 4) * (4 * CAP), 4 * CAP)
+        first = pl.multiple_of((((me >> 2) + c) & 3) * (4 * CAP), 4 * CAP)
         rows = pl.ds(first, 4 * CAP)
         r = lax.broadcasted_iota(jnp.int32, (4 * CAP, 128), 0) + first
         source = div48(r)
@@ -306,6 +307,12 @@
             fwd_copy(a, d).wait_recv()
 
         kv_copy(a).start()
+
+    @pl.loop(0, routes // 256)
+    def _(c):
+        rows = pl.ds(pl.multiple_of(c * 256, 256), 256)
+        f = lax.broadcasted_iota(jnp.int32, (count, 128), 0)
+        dest_ref[rows, :] = dot(mixed_ref[rows, :], dest_weight(f))
 
     @pl.loop(4, 4 * OWN)
     def _(n):
@@ -556,6 +563,7 @@
             vmem((routes, 3 * HS), BF16),
             vmem((routes, HS), BF16),
             vmem((routes, HS), BF16),
+            vmem((routes, 5 * top), BF16),
             vmem((8, routes), F32),
             vmem((OWN, SPAN, WIDE), BF16),
             vmem((OWN, SPAN, WIDE), BF16),

time: 89.2 us -> 89.1 us (level)
  no operation moved by 1% of the time
where the time goes in v4:
time: 89.1 us; the launch traced here: 87.7 us
  Pallas kernels  87 us (98%)
    pallas_call x1, Pallas kernels, per_device(): pl.pallas_call(kernel, out_shape=(jax.ShapeDtypeStruct((routes, WIDE), BF...  83.8 us
    pallas_call x1, Pallas kernels, per_device(): pl.pallas_call(home_kernel, out_shape=(jax.ShapeDtypeStruct((routes, HS),...  3.17 us

profile of v4, /device:TPU:97, one launch (start us, length us, event | category | flops | bytes accessed | tf_op | source)
XLA Modules:
  0.0 87.7 jit_solution(3422235235445814421)
XLA Ops:
  0.6 0.0 copy-start
  0.6 0.0 copy-start.1
  0.7 83.8 %shard_map.85 = (bf16[1536,512]{1,0:T(8,128)(2,1)S(1)}, bf16[4,2,768,256]{3,2,1,0:T(8,128)(2,1)S(1)}, f32[1536,128]{1,0:T(8,128)S(1)}, f32[1536,128]{1,0:T(8,128)S(1)}) custom-call(bf16[1536,384]{1,0:T(8,128)(2,1)} %bitcast.12, bf16[1536,128]{1,0:T(8,128)(2,1)} %bitcast.8, s32[8,192]{1,0:T(8,128)} %bitcast.13, s32[8,192]{1,0:T(8,128)} %bitcast.14, ...), custom_call_target="tpu_custom_call" | custom-call | tf_op jit(solution)/shard_map/pallas_call | solution.py:551
  84.5 0.0 copy-done
  84.5 0.0 copy-done.1
  84.5 3.2 %shard_map.86 = (bf16[1536,128]{1,0:T(8,128)(2,1)}, bf16[1536,384]{1,0:T(8,128)(2,1)}, f32[8,192]{1,0:T(8,128)}) custom-call(bf16[1536,512]{1,0:T(8,128)(2,1)S(1)} %get-tuple-element.10.routes_ref, bf16[4,2,768,256]{3,2,1,0:T(8,128)(2,1)S(1)} %get-tuple-element.11.last_ref, f32[1536,128]{1,0:T(8,128)S(1)} %get-tuple-element.12.dest_ref, ...), custom_call_target="tpu_custom_call" | custom-call | tf_op jit(solution)/shard_map/pallas_call | solution.py:617
Async XLA Ops:
  0.6 83.8 %copy-start = (bf16[192,8,128]{2,1,0:T(8,128)(2,1)S(1)}, bf16[192,8,128]{2,1,0:T(8,128)(2,1)}, u32[]{:S(2)}) copy-start(bf16[192,8,128]{2,1,0:T(8,128)(2,1)} %param.11) | copy-start | bytes 1179652
  0.6 83.8 %copy-start.1 = (f32[192,8]{0,1:T(8,128)S(1)}, f32[192,8]{0,1:T(8,128)}, u32[]{:S(2)}) copy-start(f32[192,8]{0,1:T(8,128)} %param.9) | copy-start | bytes 18436

commit v5 on v4

--- a/solution.py
+++ b/solution.py
@@ -455,7 +455,7 @@
 
     @pl.loop(0, OWN - 1)
     def _(a):
-        @pl.when(a == OWN - 2)
+        @pl.when(a == 1)
         def _():
             finish(OWN - 1)
 

time: 89.1 us -> 89.1 us (level)
  no operation moved by 1% of the time
where the time goes in v5:
time: 89.1 us; the launch traced here: 87.7 us
  Pallas kernels  87 us (98%)
    pallas_call x1, Pallas kernels, per_device(): pl.pallas_call(kernel, out_shape=(jax.ShapeDtypeStruct((routes, WIDE), BF...  83.8 us
    pallas_call x1, Pallas kernels, per_device(): pl.pallas_call(home_kernel, out_shape=(jax.ShapeDtypeStruct((routes, HS),...  3.17 us

profile of v5, /device:TPU:97, one launch (start us, length us, event | category | flops | bytes accessed | tf_op | source)
XLA Modules:
  0.0 87.7 jit_solution(15308331923150943095)
XLA Ops:
  0.6 0.0 copy-start
  0.6 0.0 copy-start.1
  0.7 83.8 %shard_map.85 = (bf16[1536,512]{1,0:T(8,128)(2,1)S(1)}, bf16[4,2,768,256]{3,2,1,0:T(8,128)(2,1)S(1)}, f32[1536,128]{1,0:T(8,128)S(1)}, f32[1536,128]{1,0:T(8,128)S(1)}) custom-call(bf16[1536,384]{1,0:T(8,128)(2,1)} %bitcast.12, bf16[1536,128]{1,0:T(8,128)(2,1)} %bitcast.8, s32[8,192]{1,0:T(8,128)} %bitcast.13, s32[8,192]{1,0:T(8,128)} %bitcast.14, ...), custom_call_target="tpu_custom_call" | custom-call | tf_op jit(solution)/shard_map/pallas_call | solution.py:551
  84.5 0.0 copy-done
  84.5 0.0 copy-done.1
  84.5 3.2 %shard_map.86 = (bf16[1536,128]{1,0:T(8,128)(2,1)}, bf16[1536,384]{1,0:T(8,128)(2,1)}, f32[8,192]{1,0:T(8,128)}) custom-call(bf16[1536,512]{1,0:T(8,128)(2,1)S(1)} %get-tuple-element.10.routes_ref, bf16[4,2,768,256]{3,2,1,0:T(8,128)(2,1)S(1)} %get-tuple-element.11.last_ref, f32[1536,128]{1,0:T(8,128)S(1)} %get-tuple-element.12.dest_ref, ...), custom_call_target="tpu_custom_call" | custom-call | tf_op jit(solution)/shard_map/pallas_call | solution.py:617
Async XLA Ops:
  0.6 83.8 %copy-start = (bf16[192,8,128]{2,1,0:T(8,128)(2,1)S(1)}, bf16[192,8,128]{2,1,0:T(8,128)(2,1)}, u32[]{:S(2)}) copy-start(bf16[192,8,128]{2,1,0:T(8,128)(2,1)} %param.11) | copy-start | bytes 1179652
  0.6 83.8 %copy-start.1 = (f32[192,8]{0,1:T(8,128)S(1)}, f32[192,8]{0,1:T(8,128)}, u32[]{:S(2)}) copy-start(f32[192,8]{0,1:T(8,128)} %param.9) | copy-start | bytes 18436

commit v6 on v4

--- a/solution.py
+++ b/solution.py
@@ -16,7 +16,7 @@
 WIDE = 4 * HS
 QT = 256
 WIN = 1152
-KC = 384
+KC = 544
 MASKED = -1e30
 F32 = jnp.float32
 BF16 = jnp.bfloat16

time: 89.1 us -> 89.1 us (level)
  no operation moved by 1% of the time
where the time goes in v6:
time: 89.1 us; the launch traced here: 87.7 us
  Pallas kernels  87 us (98%)
    pallas_call x1, Pallas kernels, per_device(): pl.pallas_call(kernel, out_shape=(jax.ShapeDtypeStruct((routes, WIDE), BF...  83.8 us
    pallas_call x1, Pallas kernels, per_device(): pl.pallas_call(home_kernel, out_shape=(jax.ShapeDtypeStruct((routes, HS),...  3.17 us

profile of v6, /device:TPU:97, one launch (start us, length us, event | category | flops | bytes accessed | tf_op | source)
XLA Modules:
  0.0 87.7 jit_solution(14690844625126450476)
XLA Ops:
  0.6 0.0 copy-start
  0.6 0.0 copy-start.1
  0.7 83.8 %shard_map.85 = (bf16[1536,512]{1,0:T(8,128)(2,1)S(1)}, bf16[4,2,768,256]{3,2,1,0:T(8,128)(2,1)S(1)}, f32[1536,128]{1,0:T(8,128)S(1)}, f32[1536,128]{1,0:T(8,128)S(1)}) custom-call(bf16[1536,384]{1,0:T(8,128)(2,1)} %bitcast.12, bf16[1536,128]{1,0:T(8,128)(2,1)} %bitcast.8, s32[8,192]{1,0:T(8,128)} %bitcast.13, s32[8,192]{1,0:T(8,128)} %bitcast.14, ...), custom_call_target="tpu_custom_call" | custom-call | tf_op jit(solution)/shard_map/pallas_call | solution.py:551
  84.5 0.0 copy-done
  84.5 0.0 copy-done.1
  84.5 3.2 %shard_map.86 = (bf16[1536,128]{1,0:T(8,128)(2,1)}, bf16[1536,384]{1,0:T(8,128)(2,1)}, f32[8,192]{1,0:T(8,128)}) custom-call(bf16[1536,512]{1,0:T(8,128)(2,1)S(1)} %get-tuple-element.10.routes_ref, bf16[4,2,768,256]{3,2,1,0:T(8,128)(2,1)S(1)} %get-tuple-element.11.last_ref, f32[1536,128]{1,0:T(8,128)S(1)} %get-tuple-element.12.dest_ref, ...), custom_call_target="tpu_custom_call" | custom-call | tf_op jit(solution)/shard_map/pallas_call | solution.py:617
Async XLA Ops:
  0.6 83.8 %copy-start = (bf16[192,8,128]{2,1,0:T(8,128)(2,1)S(1)}, bf16[192,8,128]{2,1,0:T(8,128)(2,1)}, u32[]{:S(2)}) copy-start(bf16[192,8,128]{2,1,0:T(8,128)(2,1)} %param.11) | copy-start | bytes 1179652
  0.6 83.8 %copy-start.1 = (f32[192,8]{0,1:T(8,128)S(1)}, f32[192,8]{0,1:T(8,128)}, u32[]{:S(2)}) copy-start(f32[192,8]{0,1:T(8,128)} %param.9) | copy-start | bytes 18436
